TPU v7x, 256 devices: a whole 4x4x8 slice. The times are simulated.
256 devices in a mesh: blk: 64 (over y_lo, z, x), rep: 4 (over y_hi, core).
Axes of the slice: x: 4, y: 4 (y_hi: 2, y_lo: 2; y = y_hi * 2 + y_lo), z: 8, core: 2. Of those that a mesh axis runs over, the one named last changes fastest.
Arguments:
- points: bfloat16 [49152, 1024], P('blk'), may hold values from -6 to 6
- w_in: bfloat16 [1024, 512], replicated, may hold values from -0.1875 to 0.1875
- b_in: float32 [512], replicated, may hold values from -3 to 3
- w_out: bfloat16 [512, 64], replicated, may hold values from -0.25 to 0.25
- inv_scale: float32 [64], replicated, may hold values from 0.05 to 0.5
- solves: bfloat16 [64, 49152], P(None, 'blk'), may hold values from -1 to 1
- probes: bfloat16 [64, 49152], P(None, 'blk'), may hold values from -1 to 1
Outputs:
- feat_grad: float32 [64, 49152], P(None, ('blk', 'rep'))
- grad_w_in: float32 [1024, 512], replicated
- grad_b_in: float32 [512], replicated
- grad_w_out: float32 [512, 64], replicated
All inputs are finite; a program needn't handle non-finite values.
Results may differ from a plain program's by a relative error of at most 0.034.
Values may be sent and summed in bfloat16 or wider, within the bound.
A program may use at most 64 MiB of HBM per device.

v0:
```python
import math
import jax
import jax.numpy as jnp
from jax import lax
from jax.sharding import PartitionSpec as P


def shifted(block, axis, distance):
    devices = range(lax.axis_size(axis))
    route = [((i - distance) % len(devices), i) for i in devices]
    return lax.ppermute(block, axis, route)


def cut_along(value, dim, count):
    lengths = value.shape
    blocks = value.reshape(*lengths[:dim], count, lengths[dim] // count, *lengths[dim + 1 :])
    return jnp.moveaxis(blocks, dim, 0)


def sum_at_owner(value, axis, dim):
    count = lax.axis_size(axis)
    blocks = lax.all_to_all(cut_along(value, dim, count), axis, 0, 0, tiled=True)
    return jnp.sum(blocks, axis=0)


def couple(own_y, own_pair, own_sq, visitor, feat):
    vis_y = visitor[:feat]
    vis_pair = visitor[feat:]
    vis_sq = jnp.sum(jnp.square(vis_y.astype(jnp.float32)), axis=0)
    cross = lax.dot_general(
        own_y, vis_y, (((0,), (0,)), ((), ())), preferred_element_type=jnp.float32
    )
    kernel = jnp.exp(-0.5 * (own_sq[:, None] + vis_sq[None, :] - 2.0 * cross))
    coupling = lax.dot_general(
        own_pair, vis_pair, (((0,), (0,)), ((), ())), preferred_element_type=jnp.float32
    )
    weight_b = (coupling * kernel).astype(jnp.bfloat16)
    totals = jnp.sum(weight_b.astype(jnp.float32), axis=1)
    pull = lax.dot_general(
        vis_y, weight_b, (((1,), (1,)), ((), ())), preferred_element_type=jnp.float32
    )
    return (totals, pull)


def on_device(points, w_in, b_in, w_out, inv_scale, solves, probes):
    feat = w_out.shape[1]
    reps = lax.axis_size("rep")
    blocks = lax.axis_size("blk")
    rep_index = lax.axis_index("rep")
    rows = points.shape[0]
    quarter = rows // reps
    first = rep_index * quarter
    npts = rows * blocks
    levels = reps.bit_length() - 1
    own_points = lax.dynamic_slice_in_dim(points, first, quarter, 0)
    hidden = jnp.tanh(jnp.dot(points, w_in, preferred_element_type=jnp.float32) + b_in).astype(
        jnp.bfloat16
    )
    pre = lax.dot_general(
        w_out, hidden, (((0,), (1,)), ((), ())), preferred_element_type=jnp.float32
    )
    hidden, scaled = (hidden, (pre * inv_scale[:, None]).astype(jnp.bfloat16))
    own_hidden = lax.dynamic_slice_in_dim(hidden, first, quarter, 0)
    own_pair = jnp.concatenate([solves, probes], axis=0)
    own_sq = jnp.sum(jnp.square(scaled.astype(jnp.float32)), axis=0)
    scaled32 = scaled.astype(jnp.float32)
    visitor = jnp.concatenate([scaled, probes, solves], axis=0)
    for bit in range(levels):
        moved = shifted(visitor, "blk", -(1 << bit))
        visitor = jnp.where(rep_index // (1 << bit) % 2 == 1, moved, visitor)

    def accumulate(state, vis):
        totals, pull = couple(scaled, own_pair, own_sq, vis, feat)
        return (state[0] + totals, state[1] + pull)

    init = (jnp.zeros((rows,), jnp.float32), jnp.zeros((feat, rows), jnp.float32))
    steps = blocks // reps
    behind = shifted(visitor, "blk", reps)

    def advance_both(index, carry):
        state, ahead_vis, behind_vis = carry
        state = accumulate(accumulate(state, ahead_vis), behind_vis)
        ahead_vis = shifted(ahead_vis, "blk", -reps)
        behind_vis = shifted(behind_vis, "blk", reps)
        return (state, ahead_vis, behind_vis)

    state, ahead_vis, behind_vis = lax.fori_loop(
        0, steps // 2 - 1, advance_both, (init, visitor, behind)
    )
    state = accumulate(accumulate(state, ahead_vis), behind_vis)
    totals, pull = state
    drift = pull - scaled32 * totals[None, :]
    summed = sum_at_owner(drift, "rep", 1)
    feat_grad = summed * inv_scale[:, None]
    grad_b16 = feat_grad.astype(jnp.bfloat16)
    back = lax.dot_general(
        grad_b16, w_out, (((0,), (1,)), ((), ())), preferred_element_type=jnp.float32
    )
    hid32 = own_hidden.astype(jnp.float32)
    pre_grad = back * (1.0 - hid32 * hid32)
    norm = 1.0 / math.sqrt(npts)
    term_w_in = (
        lax.dot_general(
            own_points,
            pre_grad.astype(jnp.bfloat16),
            (((0,), (0,)), ((), ())),
            preferred_element_type=jnp.float32,
        )
        * norm
    )
    term_b_in = jnp.sum(pre_grad, axis=0) * norm
    term_w_out = (
        lax.dot_general(
            own_hidden, grad_b16, (((0,), (1,)), ((), ())), preferred_element_type=jnp.float32
        )
        * norm
    )
    grad_w_in, grad_b_in, grad_w_out = lax.psum((term_w_in, term_b_in, term_w_out), ("blk", "rep"))
    return (feat_grad, grad_w_in, grad_b_in, grad_w_out)


def solution(mesh):
    in_specs = (P("blk", None), P(), P(), P(), P(), P(None, "blk"), P(None, "blk"))
    out_specs = (P(None, ("blk", "rep")), P(), P(), P())
    return jax.shard_map(
        on_device, mesh=mesh, in_specs=in_specs, out_specs=out_specs, check_vma=False
    )
```

profile of v0, /device:TPU:2, one launch (start us, length us, event | category | flops | bytes accessed | tf_op | source)
XLA Modules:
  0.0 443.5 jit_solution(13951835075255544906)
XLA Ops:
  8.6 2.2 tanh_convert_fusion
  13.6 2.3 collective-permute-start.2
  16.0 6.5 %collective-permute-done.2 = bf16[192,768]{1,0:T(8,128)(2,1)S(1)} collective-permute-done((bf16[192,768]{1,0:T(8,128)(2,1)S(1)}, bf16[192,768]{1,0:T(8,128)(2,1)S(1)}, u32[]{:S(2)}, u32[]{:S(2)}) %collective-permute-start.2) | collective-permute-done | bytes 294944 | tf_op jit(solution)/shard_map/ppermute | solution.py:11
  23.4 12.7 %collective-permute-start.3 = (bf16[192,768]{1,0:T(8,128)(2,1)S(1)}, bf16[192,768]{1,0:T(8,128)(2,1)S(1)}, u32[]{:S(2)}, u32[]{:S(2)}) collective-permute-start(bf16[192,768]{1,0:T(8,128)(2,1)S(1)} %broadcast_select_fusion), channel_id=1, source_target_pairs={{8,0},{12,4},{16,8},{20,12},{24,16},{28,20},{32,24},{36,28},{40,32... | collective-permute-start | bytes 884744 | tf_op jit(solution)/shard_map/ppermute | solution.py:11
  36.2 5.4 %collective-permute-done.3 = bf16[192,768]{1,0:T(8,128)(2,1)S(1)} collective-permute-done((bf16[192,768]{1,0:T(8,128)(2,1)S(1)}, bf16[192,768]{1,0:T(8,128)(2,1)S(1)}, u32[]{:S(2)}, u32[]{:S(2)}) %collective-permute-start.3) | collective-permute-done | bytes 294944 | tf_op jit(solution)/shard_map/ppermute | solution.py:11
  42.3 9.3 %collective-permute-done.4 = bf16[192,768]{1,0:T(8,128)(2,1)} collective-permute-done((bf16[192,768]{1,0:T(8,128)(2,1)}, bf16[192,768]{1,0:T(8,128)(2,1)}, u32[]{:S(2)}, u32[]{:S(2)}) %collective-permute-start.4) | collective-permute-done | bytes 294944 | tf_op jit(solution)/shard_map/ppermute | solution.py:11
  51.7 93.9 %while.17 = (s32[]{:T(128)}, f32[768]{0:T(1024)S(1)}, f32[64,768]{1,0:T(8,128)}, bf16[192,768]{1,0:T(8,128)(2,1)}, bf16[192,768]{1,0:T(8,128)(2,1)}, /*index=5*/...) while((s32[]{:T(128)}, f32[768]{0:T(1024)S(1)}, ...), condition=%wide.region_6.7_spmd.clone, body=%wide.region_1.6_spmd.clone.sunk | while | flops 613858560 | bytes 20095168 | solution.py:87
  53.6 2.0 collective-permute-start.1
  56.7 1.8 convert_reduce_fusion.6
  61.3 1.9 fusion.79
  64.3 2.1 collective-permute-start
  68.4 1.8 convert_reduce_fusion.6
  73.1 2.0 fusion.79
  77.3 3.0 collective-permute-start
  82.3 1.8 convert_reduce_fusion.6
  86.9 2.0 fusion.79
  91.1 3.0 collective-permute-start
  100.8 2.0 fusion.79
  104.9 3.0 collective-permute-start
  114.6 2.0 fusion.79
  118.8 3.0 collective-permute-start
  128.5 2.0 fusion.79
  132.6 3.0 collective-permute-start
  142.3 2.0 fusion.79
  149.4 1.8 convert_reduce_fusion.3
  152.5 1.9 convert_reduce_fusion.2
  156.8 4.1 all-to-all-start
  160.9 7.5 %all-to-all-done = f32[4,64,192]{2,1,0:T(8,128)S(1)} async-done(((f32[4,64,192]{2,1,0:T(8,128)}), f32[4,64,192]{2,1,0:T(8,128)S(1)}, u32[]{:S(2)}, u32[]{:S(2)}) %all-to-all-start) | async-done | bytes 196640 | tf_op jit(solution)/shard_map/all_to_all | solution.py:22
  169.6 1.8 convolution_multiply_fusion
  171.5 78.0 %psum.22 = f32[512]{0:T(512)} all-reduce(f32[512]{0:T(512)S(1)} %broadcast_multiply_fusion.1), channel_id=1, replica_groups=mesh['blk'=64,'rep'=4] {'blk','rep'}, use_global_device_ids=true, to_apply=%region_14.15 | all-reduce | flops 512 | bytes 4096 | tf_op jit(solution)/shard_map/psum | solution.py:118
  249.5 183.4 %all-reduce.3.cloned.1.call-done = (f32[1024,512]{1,0:T(8,128)}, f32[512,64]{0,1:T(8,128)}) async-done(((f32[1024,512]{1,0:T(8,128)}, f32[512,64]{0,1:T(8,128)}), (f32[1024,512]{1,0:T(8,128)}, f32[512,64]{0,1:T(8,128)})) %all-reduce.3.cloned.1.call-update) | async-done | bytes 2228240 | tf_op jit(solution)/shard_map/psum | solution.py:118
  432.9 3.1 copy.32
  (130 shorter events, 70.0 us)
Async XLA Ops:
  7.2 1.4 copy-start
  7.2 4.5 %copy-start.8 = (bf16[512,64]{0,1:T(8,128)(2,1)S(1)}, bf16[512,64]{0,1:T(8,128)(2,1)}, u32[]{:S(2)}) copy-start(bf16[512,64]{0,1:T(8,128)(2,1)} %param.12) | copy-start | bytes 196612
  7.2 4.5 %copy-start.10 = (f32[64]{0:T(128)S(1)}, f32[64]{0:T(128)}, u32[]{:S(2)}) copy-start(f32[64]{0:T(128)} %param.13) | copy-start | bytes 772
  7.2 5.5 %copy-start.4 = (bf16[64,768]{1,0:T(8,128)(2,1)S(1)}, bf16[64,768]{1,0:T(8,128)(2,1)}, u32[]{:S(2)}) copy-start(bf16[64,768]{1,0:T(8,128)(2,1)} %param.14) | copy-start | bytes 294916
  8.6 4.1 copy-start.5
  10.8 0.9 copy-start.2
  13.6 8.8 %collective-permute-start.2 = (bf16[192,768]{1,0:T(8,128)(2,1)S(1)}, bf16[192,768]{1,0:T(8,128)(2,1)S(1)}, u32[]{:S(2)}, u32[]{:S(2)}) collective-permute-start(bf16[192,768]{1,0:T(8,128)(2,1)S(1)} %pad_maximum_fusion), channel_id=1, source_target_pairs={{4,0},{8,4},{12,8},{16,12},{20,16},{24,20},{28,24},{32,28},{36,32}... | collective-permute-start | bytes 884744 | tf_op jit(solution)/shard_map/ppermute | solution.py:11
  23.4 18.1 %collective-permute-start.3 = (bf16[192,768]{1,0:T(8,128)(2,1)S(1)}, bf16[192,768]{1,0:T(8,128)(2,1)S(1)}, u32[]{:S(2)}, u32[]{:S(2)}) collective-permute-start(bf16[192,768]{1,0:T(8,128)(2,1)S(1)} %broadcast_select_fusion), channel_id=1, source_target_pairs={{8,0},{12,4},{16,8},{20,12},{24,16},{28,20},{32,24},{36,28},{40,32... | collective-permute-start | bytes 884744 | tf_op jit(solution)/shard_map/ppermute | solution.py:11
  42.3 9.4 %collective-permute-start.4 = (bf16[192,768]{1,0:T(8,128)(2,1)}, bf16[192,768]{1,0:T(8,128)(2,1)}, u32[]{:S(2)}, u32[]{:S(2)}) collective-permute-start(bf16[192,768]{1,0:T(8,128)(2,1)} %broadcast_select_fusion.1), channel_id=1, source_target_pairs={{240,0},{244,4},{248,8},{252,12},{0,16},{4,20},{8,24},{12,28},{16,... | collective-permute-start | bytes 884744 | tf_op jit(solution)/shard_map/ppermute | solution.py:11
  52.6 10.7 %collective-permute-start = (bf16[192,768]{1,0:T(8,128)(2,1)S(1)}, bf16[192,768]{1,0:T(8,128)(2,1)}, u32[]{:S(2)}, u32[]{:S(2)}) collective-permute-start(bf16[192,768]{1,0:T(8,128)(2,1)S(1)} %copy.23), channel_id=1, source_target_pairs={{16,0},{20,4},{24,8},{28,12},{32,16},{36,20},{40,24},{44,28},{48,3... | collective-permute-start | bytes 884744 | tf_op jit(solution)/shard_map/while/body/eval_jaxpr/ppermute | solution.py:11
  53.6 9.7 %collective-permute-start.1 = (bf16[192,768]{1,0:T(8,128)(2,1)S(1)}, bf16[192,768]{1,0:T(8,128)(2,1)}, u32[]{:S(2)}, u32[]{:S(2)}) collective-permute-start(bf16[192,768]{1,0:T(8,128)(2,1)S(1)} %copy.24), channel_id=1, source_target_pairs={{240,0},{244,4},{248,8},{252,12},{0,16},{4,20},{8,24},{12,28},{16,... | collective-permute-start | bytes 884744 | tf_op jit(solution)/shard_map/while/body/eval_jaxpr/ppermute | solution.py:11
  64.3 10.9 %collective-permute-start = (bf16[192,768]{1,0:T(8,128)(2,1)S(1)}, bf16[192,768]{1,0:T(8,128)(2,1)}, u32[]{:S(2)}, u32[]{:S(2)}) collective-permute-start(bf16[192,768]{1,0:T(8,128)(2,1)S(1)} %copy.23), channel_id=1, source_target_pairs={{16,0},{20,4},{24,8},{28,12},{32,16},{36,20},{40,24},{44,28},{48,3... | collective-permute-start | bytes 884744 | tf_op jit(solution)/shard_map/while/body/eval_jaxpr/ppermute | solution.py:11
  67.4 8.9 %collective-permute-start.1 = (bf16[192,768]{1,0:T(8,128)(2,1)S(1)}, bf16[192,768]{1,0:T(8,128)(2,1)}, u32[]{:S(2)}, u32[]{:S(2)}) collective-permute-start(bf16[192,768]{1,0:T(8,128)(2,1)S(1)} %copy.24), channel_id=1, source_target_pairs={{240,0},{244,4},{248,8},{252,12},{0,16},{4,20},{8,24},{12,28},{16,... | collective-permute-start | bytes 884744 | tf_op jit(solution)/shard_map/while/body/eval_jaxpr/ppermute | solution.py:11
  77.3 11.7 %collective-permute-start = (bf16[192,768]{1,0:T(8,128)(2,1)S(1)}, bf16[192,768]{1,0:T(8,128)(2,1)}, u32[]{:S(2)}, u32[]{:S(2)}) collective-permute-start(bf16[192,768]{1,0:T(8,128)(2,1)S(1)} %copy.23), channel_id=1, source_target_pairs={{16,0},{20,4},{24,8},{28,12},{32,16},{36,20},{40,24},{44,28},{48,3... | collective-permute-start | bytes 884744 | tf_op jit(solution)/shard_map/while/body/eval_jaxpr/ppermute | solution.py:11
  81.2 8.9 %collective-permute-start.1 = (bf16[192,768]{1,0:T(8,128)(2,1)S(1)}, bf16[192,768]{1,0:T(8,128)(2,1)}, u32[]{:S(2)}, u32[]{:S(2)}) collective-permute-start(bf16[192,768]{1,0:T(8,128)(2,1)S(1)} %copy.24), channel_id=1, source_target_pairs={{240,0},{244,4},{248,8},{252,12},{0,16},{4,20},{8,24},{12,28},{16,... | collective-permute-start | bytes 884744 | tf_op jit(solution)/shard_map/while/body/eval_jaxpr/ppermute | solution.py:11
  91.1 11.7 %collective-permute-start = (bf16[192,768]{1,0:T(8,128)(2,1)S(1)}, bf16[192,768]{1,0:T(8,128)(2,1)}, u32[]{:S(2)}, u32[]{:S(2)}) collective-permute-start(bf16[192,768]{1,0:T(8,128)(2,1)S(1)} %copy.23), channel_id=1, source_target_pairs={{16,0},{20,4},{24,8},{28,12},{32,16},{36,20},{40,24},{44,28},{48,3... | collective-permute-start | bytes 884744 | tf_op jit(solution)/shard_map/while/body/eval_jaxpr/ppermute | solution.py:11
  95.0 8.9 %collective-permute-start.1 = (bf16[192,768]{1,0:T(8,128)(2,1)S(1)}, bf16[192,768]{1,0:T(8,128)(2,1)}, u32[]{:S(2)}, u32[]{:S(2)}) collective-permute-start(bf16[192,768]{1,0:T(8,128)(2,1)S(1)} %copy.24), channel_id=1, source_target_pairs={{240,0},{244,4},{248,8},{252,12},{0,16},{4,20},{8,24},{12,28},{16,... | collective-permute-start | bytes 884744 | tf_op jit(solution)/shard_map/while/body/eval_jaxpr/ppermute | solution.py:11
  104.9 11.7 %collective-permute-start = (bf16[192,768]{1,0:T(8,128)(2,1)S(1)}, bf16[192,768]{1,0:T(8,128)(2,1)}, u32[]{:S(2)}, u32[]{:S(2)}) collective-permute-start(bf16[192,768]{1,0:T(8,128)(2,1)S(1)} %copy.23), channel_id=1, source_target_pairs={{16,0},{20,4},{24,8},{28,12},{32,16},{36,20},{40,24},{44,28},{48,3... | collective-permute-start | bytes 884744 | tf_op jit(solution)/shard_map/while/body/eval_jaxpr/ppermute | solution.py:11
  108.9 8.9 %collective-permute-start.1 = (bf16[192,768]{1,0:T(8,128)(2,1)S(1)}, bf16[192,768]{1,0:T(8,128)(2,1)}, u32[]{:S(2)}, u32[]{:S(2)}) collective-permute-start(bf16[192,768]{1,0:T(8,128)(2,1)S(1)} %copy.24), channel_id=1, source_target_pairs={{240,0},{244,4},{248,8},{252,12},{0,16},{4,20},{8,24},{12,28},{16,... | collective-permute-start | bytes 884744 | tf_op jit(solution)/shard_map/while/body/eval_jaxpr/ppermute | solution.py:11
  118.8 11.7 %collective-permute-start = (bf16[192,768]{1,0:T(8,128)(2,1)S(1)}, bf16[192,768]{1,0:T(8,128)(2,1)}, u32[]{:S(2)}, u32[]{:S(2)}) collective-permute-start(bf16[192,768]{1,0:T(8,128)(2,1)S(1)} %copy.23), channel_id=1, source_target_pairs={{16,0},{20,4},{24,8},{28,12},{32,16},{36,20},{40,24},{44,28},{48,3... | collective-permute-start | bytes 884744 | tf_op jit(solution)/shard_map/while/body/eval_jaxpr/ppermute | solution.py:11
  122.7 8.9 %collective-permute-start.1 = (bf16[192,768]{1,0:T(8,128)(2,1)S(1)}, bf16[192,768]{1,0:T(8,128)(2,1)}, u32[]{:S(2)}, u32[]{:S(2)}) collective-permute-start(bf16[192,768]{1,0:T(8,128)(2,1)S(1)} %copy.24), channel_id=1, source_target_pairs={{240,0},{244,4},{248,8},{252,12},{0,16},{4,20},{8,24},{12,28},{16,... | collective-permute-start | bytes 884744 | tf_op jit(solution)/shard_map/while/body/eval_jaxpr/ppermute | solution.py:11
  132.6 11.7 %collective-permute-start = (bf16[192,768]{1,0:T(8,128)(2,1)S(1)}, bf16[192,768]{1,0:T(8,128)(2,1)}, u32[]{:S(2)}, u32[]{:S(2)}) collective-permute-start(bf16[192,768]{1,0:T(8,128)(2,1)S(1)} %copy.23), channel_id=1, source_target_pairs={{16,0},{20,4},{24,8},{28,12},{32,16},{36,20},{40,24},{44,28},{48,3... | collective-permute-start | bytes 884744 | tf_op jit(solution)/shard_map/while/body/eval_jaxpr/ppermute | solution.py:11
  136.6 8.9 %collective-permute-start.1 = (bf16[192,768]{1,0:T(8,128)(2,1)S(1)}, bf16[192,768]{1,0:T(8,128)(2,1)}, u32[]{:S(2)}, u32[]{:S(2)}) collective-permute-start(bf16[192,768]{1,0:T(8,128)(2,1)S(1)} %copy.24), channel_id=1, source_target_pairs={{240,0},{244,4},{248,8},{252,12},{0,16},{4,20},{8,24},{12,28},{16,... | collective-permute-start | bytes 884744 | tf_op jit(solution)/shard_map/while/body/eval_jaxpr/ppermute | solution.py:11
  152.5 1.9 copy-start.1
  154.4 14.0 %copy-start.11 = (f32[64]{0:T(128)S(1)}, f32[64]{0:T(128)}, u32[]{:S(2)}) copy-start(f32[64]{0:T(128)} %param.13) | copy-start | bytes 772
  154.4 14.1 %copy-start.3 = (bf16[768,512]{1,0:T(8,128)(2,1)S(1)}, bf16[768,512]{1,0:T(8,128)(2,1)}, u32[]{:S(2)}) copy-start(bf16[768,512]{1,0:T(8,128)(2,1)} %copy-done.2) | copy-start | bytes 2359300
  154.4 14.1 %copy-start.9 = (bf16[512,64]{0,1:T(8,128)(2,1)S(1)}, bf16[512,64]{0,1:T(8,128)(2,1)}, u32[]{:S(2)}) copy-start(bf16[512,64]{0,1:T(8,128)(2,1)} %param.12) | copy-start | bytes 196612
  156.8 11.7 %all-to-all-start = ((f32[4,64,192]{2,1,0:T(8,128)}), f32[4,64,192]{2,1,0:T(8,128)S(1)}, u32[]{:S(2)}, u32[]{:S(2)}) async-start(f32[4,64,192]{2,1,0:T(8,128)} %bitcast.31), calls=%async_computation | async-start | bytes 524288 | tf_op jit(solution)/shard_map/all_to_all | solution.py:22
  160.9 272.0 %all-reduce.3.cloned.1.call-start = ((), (), s32[]{:S(2)}) async-start(), calls=%async_computation.1 | async-start | bytes 4456448 | tf_op jit(solution)/shard_map/psum | solution.py:118
  168.5 2.9 copy-start.6
  432.9 3.1 copy-start.7
Sparse Core Ops, SparseCore 0:
  171.6 261.2 all-reduce.2
where the time goes:
time: 445 us; the launch traced here: 443 us
  waiting for transfers between devices  219 us (49%)
  blocking collectives  78 us (18%)
  matrix products  68.9 us (15%)
  starting transfers between devices  38.3 us (9%)
  local copies, waits for them, and re-layouts  20.5 us (5%)
  between operations  14.2 us (3%)
    psum x1, waiting for transfers between devices, on_device(): lax.psum((term_w_in, term_b_in, term_w_out), ('blk', 'rep'))  183 us
    psum x1, blocking collectives, on_device(): lax.psum((term_w_in, term_b_in, term_w_out), ('blk', 'rep'))  78 us
    ppermute x17, starting transfers between devices, shifted(): return lax.ppermute(block, axis, route)  34.2 us
    ppermute x17, waiting for transfers between devices, shifted(): return lax.ppermute(block, axis, route)  28.2 us
    dot_general x16, matrix products, couple(): lax.dot_general(own_y, vis_y, (((0,), (0,)), ((), ())), preferred_element...  28.1 us
    dot_general x16, matrix products, couple(): lax.dot_general(vis_y, weight_b, (((1,), (1,)), ((), ())), preferred_elem...  23.8 us
    while x14, local copies, waits for them, and re-layouts  13.5 us
    dot_general x16, matrix products, couple(): lax.dot_general(own_pair, vis_pair, (((0,), (0,)), ((), ())), preferred_e...  10.8 us
  transfers between devices with their start and end apart: 19, of which 11 were waited for; matrix products, arithmetic and copies ran while one was open for 14% of the time, Pallas kernels for 0%

commit v1 on v0

--- a/solution.py
+++ b/solution.py
@@ -115,7 +115,9 @@
         )
         * norm
     )
-    grad_w_in, grad_b_in, grad_w_out = lax.psum((term_w_in, term_b_in, term_w_out), ("blk", "rep"))
+    grad_w_in, grad_b_in, grad_w_out = lax.psum(
+        lax.psum((term_w_in, term_b_in, term_w_out), "rep"), "blk"
+    )
     return (feat_grad, grad_w_in, grad_b_in, grad_w_out)
 
 

time: 445 us -> 848 us (1.91)
  waiting for transfers between devices: 219 us -> 536 us
  blocking collectives: 78 us -> 162 us
    psum x1 -> x2, waiting for transfers between devices: 183 us -> 501 us  [the longest x1 436 us: on_device(): lax.psum(lax.psum((term_w_in, term_b_in, term_w_out), 'rep'), 'blk')]
    psum x1 -> x2, blocking collectives: 78 us -> 162 us  [the longest x1 154 us: on_device(): lax.psum(lax.psum((term_w_in, term_b_in, term_w_out), 'rep'), 'blk')]
  transfers between devices with their start and end apart: 19 -> 20, of which waited for: 11 -> 12; matrix products, arithmetic and copies ran while one was open for 14% -> 7% of each run, Pallas kernels for 0% -> 0%
where the time goes in v1:
time: 848 us; the launch traced here: 845 us
  waiting for transfers between devices  536 us (63%)
  blocking collectives  162 us (19%)
  matrix products  68.9 us (8%)
  starting transfers between devices  38.3 us (5%)
  local copies, waits for them, and re-layouts  20.5 us (2%)
  between operations  14.2 us (2%)
    psum x1, waiting for transfers between devices, on_device(): lax.psum(lax.psum((term_w_in, term_b_in, term_w_out), 'rep'), 'blk')  436 us
    psum x1, blocking collectives, on_device(): lax.psum(lax.psum((term_w_in, term_b_in, term_w_out), 'rep'), 'blk')  154 us
    psum x1, waiting for transfers between devices, on_device(): lax.psum((term_w_in, term_b_in, term_w_out), 'rep')  65 us
    ppermute x17, starting transfers between devices, shifted(): return lax.ppermute(block, axis, route)  34.2 us
    ppermute x17, waiting for transfers between devices, shifted(): return lax.ppermute(block, axis, route)  28.2 us
    dot_general x16, matrix products, couple(): lax.dot_general(own_y, vis_y, (((0,), (0,)), ((), ())), preferred_element...  28.1 us
    dot_general x16, matrix products, couple(): lax.dot_general(vis_y, weight_b, (((1,), (1,)), ((), ())), preferred_elem...  23.8 us
  transfers between devices with their start and end apart: 20, of which 12 were waited for; matrix products, arithmetic and copies ran while one was open for 7% of the time, Pallas kernels for 0%

profile of v1, /device:TPU:2, one launch (start us, length us, event | category | flops | bytes accessed | tf_op | source)
XLA Modules:
  0.0 844.7 jit_solution(4462361381588681237)
XLA Ops:
  8.6 2.2 tanh_convert_fusion
  13.6 2.3 collective-permute-start.2
  16.0 6.5 collective-permute-done.2
  23.4 12.7 %collective-permute-start.3 = (bf16[192,768]{1,0:T(8,128)(2,1)S(1)}, bf16[192,768]{1,0:T(8,128)(2,1)S(1)}, u32[]{:S(2)}, u32[]{:S(2)}) collective-permute-start(bf16[192,768]{1,0:T(8,128)(2,1)S(1)} %broadcast_select_fusion), channel_id=1, source_target_pairs={{8,0},{12,4},{16,8},{20,12},{24,16},{28,20},{32,24},{36,28},{40,32... | collective-permute-start | bytes 884744 | tf_op jit(solution)/shard_map/ppermute | solution.py:11
  36.2 5.4 collective-permute-done.3
  42.3 9.3 %collective-permute-done.4 = bf16[192,768]{1,0:T(8,128)(2,1)} collective-permute-done((bf16[192,768]{1,0:T(8,128)(2,1)}, bf16[192,768]{1,0:T(8,128)(2,1)}, u32[]{:S(2)}, u32[]{:S(2)}) %collective-permute-start.4) | collective-permute-done | bytes 294944 | tf_op jit(solution)/shard_map/ppermute | solution.py:11
  51.7 93.9 %while.17 = (s32[]{:T(128)}, f32[768]{0:T(1024)S(1)}, f32[64,768]{1,0:T(8,128)}, bf16[192,768]{1,0:T(8,128)(2,1)}, bf16[192,768]{1,0:T(8,128)(2,1)}, /*index=5*/...) while((s32[]{:T(128)}, f32[768]{0:T(1024)S(1)}, ...), condition=%wide.region_6.7_spmd.clone, body=%wide.region_1.6_spmd.clone.sunk | while | flops 613858560 | bytes 20095168 | solution.py:87
  53.6 2.0 collective-permute-start.1
  56.7 1.8 convert_reduce_fusion.6
  61.3 1.9 fusion.79
  64.3 2.1 collective-permute-start
  73.1 2.0 fusion.79
  77.3 3.0 collective-permute-start
  86.9 2.0 fusion.79
  91.1 3.0 collective-permute-start
  100.8 2.0 fusion.79
  104.9 3.0 collective-permute-start
  114.6 2.0 fusion.79
  118.8 3.0 collective-permute-start
  128.5 2.0 fusion.79
  132.6 3.0 collective-permute-start
  142.3 2.0 fusion.79
  149.4 1.8 convert_reduce_fusion.3
  152.5 1.9 convert_reduce_fusion.2
  156.8 4.1 all-to-all-start
  160.9 7.5 all-to-all-done
  169.6 1.8 convolution_multiply_fusion
  171.5 65.0 %all-reduce.7.cloned.1.call-done = (f32[1024,512]{1,0:T(8,128)}, f32[512,64]{0,1:T(8,128)}) async-done(((f32[1024,512]{1,0:T(8,128)}, f32[512,64]{0,1:T(8,128)}), (f32[1024,512]{1,0:T(8,128)}, f32[512,64]{0,1:T(8,128)})) %all-reduce.7.cloned.1.call-update) | async-done | bytes 2228240 | tf_op jit(solution)/shard_map/psum | solution.py:119
  236.5 7.5 psum.44
  244.0 154.5 %psum.45 = f32[512]{0:T(512)} all-reduce(f32[512]{0:T(512)S(1)} %psum.44), channel_id=1, replica_groups=mesh['blk'=64,'rep'=4] {'blk'}, use_global_device_ids=true, to_apply=%region_16.17 | all-reduce | flops 512 | bytes 4096 | tf_op jit(solution)/shard_map/psum | solution.py:118
  398.5 435.6 %all-reduce.5.cloned.1.call-done = (f32[1024,512]{1,0:T(8,128)}, f32[512,64]{0,1:T(8,128)}) async-done(((f32[1024,512]{1,0:T(8,128)}, f32[512,64]{0,1:T(8,128)}), (f32[1024,512]{1,0:T(8,128)}, f32[512,64]{0,1:T(8,128)})) %all-reduce.5.cloned.1.call-update) | async-done | bytes 2228240 | tf_op jit(solution)/shard_map/psum | solution.py:118
  834.1 3.1 copy.34
  (134 shorter events, 73.7 us)
Async XLA Ops:
  7.2 1.4 copy-start
  7.2 4.5 copy-start.8
  7.2 4.5 copy-start.10
  7.2 5.5 copy-start.4
  8.6 4.1 copy-start.5
  10.8 0.9 copy-start.2
  13.6 8.8 %collective-permute-start.2 = (bf16[192,768]{1,0:T(8,128)(2,1)S(1)}, bf16[192,768]{1,0:T(8,128)(2,1)S(1)}, u32[]{:S(2)}, u32[]{:S(2)}) collective-permute-start(bf16[192,768]{1,0:T(8,128)(2,1)S(1)} %pad_maximum_fusion), channel_id=1, source_target_pairs={{4,0},{8,4},{12,8},{16,12},{20,16},{24,20},{28,24},{32,28},{36,32}... | collective-permute-start | bytes 884744 | tf_op jit(solution)/shard_map/ppermute | solution.py:11
  23.4 18.1 %collective-permute-start.3 = (bf16[192,768]{1,0:T(8,128)(2,1)S(1)}, bf16[192,768]{1,0:T(8,128)(2,1)S(1)}, u32[]{:S(2)}, u32[]{:S(2)}) collective-permute-start(bf16[192,768]{1,0:T(8,128)(2,1)S(1)} %broadcast_select_fusion), channel_id=1, source_target_pairs={{8,0},{12,4},{16,8},{20,12},{24,16},{28,20},{32,24},{36,28},{40,32... | collective-permute-start | bytes 884744 | tf_op jit(solution)/shard_map/ppermute | solution.py:11
  42.3 9.4 %collective-permute-start.4 = (bf16[192,768]{1,0:T(8,128)(2,1)}, bf16[192,768]{1,0:T(8,128)(2,1)}, u32[]{:S(2)}, u32[]{:S(2)}) collective-permute-start(bf16[192,768]{1,0:T(8,128)(2,1)} %broadcast_select_fusion.1), channel_id=1, source_target_pairs={{240,0},{244,4},{248,8},{252,12},{0,16},{4,20},{8,24},{12,28},{16,... | collective-permute-start | bytes 884744 | tf_op jit(solution)/shard_map/ppermute | solution.py:11
  52.6 10.7 %collective-permute-start = (bf16[192,768]{1,0:T(8,128)(2,1)S(1)}, bf16[192,768]{1,0:T(8,128)(2,1)}, u32[]{:S(2)}, u32[]{:S(2)}) collective-permute-start(bf16[192,768]{1,0:T(8,128)(2,1)S(1)} %copy.23), channel_id=1, source_target_pairs={{16,0},{20,4},{24,8},{28,12},{32,16},{36,20},{40,24},{44,28},{48,3... | collective-permute-start | bytes 884744 | tf_op jit(solution)/shard_map/while/body/eval_jaxpr/ppermute | solution.py:11
  53.6 9.7 %collective-permute-start.1 = (bf16[192,768]{1,0:T(8,128)(2,1)S(1)}, bf16[192,768]{1,0:T(8,128)(2,1)}, u32[]{:S(2)}, u32[]{:S(2)}) collective-permute-start(bf16[192,768]{1,0:T(8,128)(2,1)S(1)} %copy.24), channel_id=1, source_target_pairs={{240,0},{244,4},{248,8},{252,12},{0,16},{4,20},{8,24},{12,28},{16,... | collective-permute-start | bytes 884744 | tf_op jit(solution)/shard_map/while/body/eval_jaxpr/ppermute | solution.py:11
  64.3 10.9 %collective-permute-start = (bf16[192,768]{1,0:T(8,128)(2,1)S(1)}, bf16[192,768]{1,0:T(8,128)(2,1)}, u32[]{:S(2)}, u32[]{:S(2)}) collective-permute-start(bf16[192,768]{1,0:T(8,128)(2,1)S(1)} %copy.23), channel_id=1, source_target_pairs={{16,0},{20,4},{24,8},{28,12},{32,16},{36,20},{40,24},{44,28},{48,3... | collective-permute-start | bytes 884744 | tf_op jit(solution)/shard_map/while/body/eval_jaxpr/ppermute | solution.py:11
  67.4 8.9 %collective-permute-start.1 = (bf16[192,768]{1,0:T(8,128)(2,1)S(1)}, bf16[192,768]{1,0:T(8,128)(2,1)}, u32[]{:S(2)}, u32[]{:S(2)}) collective-permute-start(bf16[192,768]{1,0:T(8,128)(2,1)S(1)} %copy.24), channel_id=1, source_target_pairs={{240,0},{244,4},{248,8},{252,12},{0,16},{4,20},{8,24},{12,28},{16,... | collective-permute-start | bytes 884744 | tf_op jit(solution)/shard_map/while/body/eval_jaxpr/ppermute | solution.py:11
  77.3 11.7 %collective-permute-start = (bf16[192,768]{1,0:T(8,128)(2,1)S(1)}, bf16[192,768]{1,0:T(8,128)(2,1)}, u32[]{:S(2)}, u32[]{:S(2)}) collective-permute-start(bf16[192,768]{1,0:T(8,128)(2,1)S(1)} %copy.23), channel_id=1, source_target_pairs={{16,0},{20,4},{24,8},{28,12},{32,16},{36,20},{40,24},{44,28},{48,3... | collective-permute-start | bytes 884744 | tf_op jit(solution)/shard_map/while/body/eval_jaxpr/ppermute | solution.py:11
  81.2 8.9 %collective-permute-start.1 = (bf16[192,768]{1,0:T(8,128)(2,1)S(1)}, bf16[192,768]{1,0:T(8,128)(2,1)}, u32[]{:S(2)}, u32[]{:S(2)}) collective-permute-start(bf16[192,768]{1,0:T(8,128)(2,1)S(1)} %copy.24), channel_id=1, source_target_pairs={{240,0},{244,4},{248,8},{252,12},{0,16},{4,20},{8,24},{12,28},{16,... | collective-permute-start | bytes 884744 | tf_op jit(solution)/shard_map/while/body/eval_jaxpr/ppermute | solution.py:11
  91.1 11.7 %collective-permute-start = (bf16[192,768]{1,0:T(8,128)(2,1)S(1)}, bf16[192,768]{1,0:T(8,128)(2,1)}, u32[]{:S(2)}, u32[]{:S(2)}) collective-permute-start(bf16[192,768]{1,0:T(8,128)(2,1)S(1)} %copy.23), channel_id=1, source_target_pairs={{16,0},{20,4},{24,8},{28,12},{32,16},{36,20},{40,24},{44,28},{48,3... | collective-permute-start | bytes 884744 | tf_op jit(solution)/shard_map/while/body/eval_jaxpr/ppermute | solution.py:11
  95.0 8.9 %collective-permute-start.1 = (bf16[192,768]{1,0:T(8,128)(2,1)S(1)}, bf16[192,768]{1,0:T(8,128)(2,1)}, u32[]{:S(2)}, u32[]{:S(2)}) collective-permute-start(bf16[192,768]{1,0:T(8,128)(2,1)S(1)} %copy.24), channel_id=1, source_target_pairs={{240,0},{244,4},{248,8},{252,12},{0,16},{4,20},{8,24},{12,28},{16,... | collective-permute-start | bytes 884744 | tf_op jit(solution)/shard_map/while/body/eval_jaxpr/ppermute | solution.py:11
  104.9 11.7 %collective-permute-start = (bf16[192,768]{1,0:T(8,128)(2,1)S(1)}, bf16[192,768]{1,0:T(8,128)(2,1)}, u32[]{:S(2)}, u32[]{:S(2)}) collective-permute-start(bf16[192,768]{1,0:T(8,128)(2,1)S(1)} %copy.23), channel_id=1, source_target_pairs={{16,0},{20,4},{24,8},{28,12},{32,16},{36,20},{40,24},{44,28},{48,3... | collective-permute-start | bytes 884744 | tf_op jit(solution)/shard_map/while/body/eval_jaxpr/ppermute | solution.py:11
  108.9 8.9 %collective-permute-start.1 = (bf16[192,768]{1,0:T(8,128)(2,1)S(1)}, bf16[192,768]{1,0:T(8,128)(2,1)}, u32[]{:S(2)}, u32[]{:S(2)}) collective-permute-start(bf16[192,768]{1,0:T(8,128)(2,1)S(1)} %copy.24), channel_id=1, source_target_pairs={{240,0},{244,4},{248,8},{252,12},{0,16},{4,20},{8,24},{12,28},{16,... | collective-permute-start | bytes 884744 | tf_op jit(solution)/shard_map/while/body/eval_jaxpr/ppermute | solution.py:11
  118.8 11.7 %collective-permute-start = (bf16[192,768]{1,0:T(8,128)(2,1)S(1)}, bf16[192,768]{1,0:T(8,128)(2,1)}, u32[]{:S(2)}, u32[]{:S(2)}) collective-permute-start(bf16[192,768]{1,0:T(8,128)(2,1)S(1)} %copy.23), channel_id=1, source_target_pairs={{16,0},{20,4},{24,8},{28,12},{32,16},{36,20},{40,24},{44,28},{48,3... | collective-permute-start | bytes 884744 | tf_op jit(solution)/shard_map/while/body/eval_jaxpr/ppermute | solution.py:11
  122.7 8.9 %collective-permute-start.1 = (bf16[192,768]{1,0:T(8,128)(2,1)S(1)}, bf16[192,768]{1,0:T(8,128)(2,1)}, u32[]{:S(2)}, u32[]{:S(2)}) collective-permute-start(bf16[192,768]{1,0:T(8,128)(2,1)S(1)} %copy.24), channel_id=1, source_target_pairs={{240,0},{244,4},{248,8},{252,12},{0,16},{4,20},{8,24},{12,28},{16,... | collective-permute-start | bytes 884744 | tf_op jit(solution)/shard_map/while/body/eval_jaxpr/ppermute | solution.py:11
  132.6 11.7 %collective-permute-start = (bf16[192,768]{1,0:T(8,128)(2,1)S(1)}, bf16[192,768]{1,0:T(8,128)(2,1)}, u32[]{:S(2)}, u32[]{:S(2)}) collective-permute-start(bf16[192,768]{1,0:T(8,128)(2,1)S(1)} %copy.23), channel_id=1, source_target_pairs={{16,0},{20,4},{24,8},{28,12},{32,16},{36,20},{40,24},{44,28},{48,3... | collective-permute-start | bytes 884744 | tf_op jit(solution)/shard_map/while/body/eval_jaxpr/ppermute | solution.py:11
  136.6 8.9 %collective-permute-start.1 = (bf16[192,768]{1,0:T(8,128)(2,1)S(1)}, bf16[192,768]{1,0:T(8,128)(2,1)}, u32[]{:S(2)}, u32[]{:S(2)}) collective-permute-start(bf16[192,768]{1,0:T(8,128)(2,1)S(1)} %copy.24), channel_id=1, source_target_pairs={{240,0},{244,4},{248,8},{252,12},{0,16},{4,20},{8,24},{12,28},{16,... | collective-permute-start | bytes 884744 | tf_op jit(solution)/shard_map/while/body/eval_jaxpr/ppermute | solution.py:11
  152.5 1.9 copy-start.1
  154.4 14.0 %copy-start.11 = (f32[64]{0:T(128)S(1)}, f32[64]{0:T(128)}, u32[]{:S(2)}) copy-start(f32[64]{0:T(128)} %param.13) | copy-start | bytes 772
  154.4 14.1 %copy-start.3 = (bf16[768,512]{1,0:T(8,128)(2,1)S(1)}, bf16[768,512]{1,0:T(8,128)(2,1)}, u32[]{:S(2)}) copy-start(bf16[768,512]{1,0:T(8,128)(2,1)} %copy-done.2) | copy-start | bytes 2359300
  154.4 14.1 %copy-start.9 = (bf16[512,64]{0,1:T(8,128)(2,1)S(1)}, bf16[512,64]{0,1:T(8,128)(2,1)}, u32[]{:S(2)}) copy-start(bf16[512,64]{0,1:T(8,128)(2,1)} %param.12) | copy-start | bytes 196612
  156.8 11.7 %all-to-all-start = ((f32[4,64,192]{2,1,0:T(8,128)}), f32[4,64,192]{2,1,0:T(8,128)S(1)}, u32[]{:S(2)}, u32[]{:S(2)}) async-start(f32[4,64,192]{2,1,0:T(8,128)} %bitcast.31), calls=%async_computation | async-start | bytes 524288 | tf_op jit(solution)/shard_map/all_to_all | solution.py:22
  160.9 75.6 %all-reduce.7.cloned.1.call-start = ((), (), s32[]{:S(2)}) async-start(), calls=%async_computation.2 | async-start | bytes 4456448 | tf_op jit(solution)/shard_map/psum | solution.py:119
  168.5 2.9 copy-start.6
  171.5 662.6 %all-reduce.5.cloned.1.call-start = ((), (), s32[]{:S(2)}) async-start(), calls=%async_computation.1 | async-start | bytes 4456448 | tf_op jit(solution)/shard_map/psum | solution.py:118
  834.1 3.1 copy-start.7
Sparse Core Ops, SparseCore 0:
  171.6 64.8 all-reduce.6
  239.2 594.8 all-reduce.4
